TPU v7x, 32 devices: a whole 2x2x4 slice. The times are simulated.
32 devices in a mesh: ops: 4 (over z), sec: 8 (over y, x, core).
Axes of the slice: x: 2, y: 2, z: 4, core: 2. Of those that a mesh axis runs over, the one named last changes fastest.
Arguments:
- wavefunction: float32 [512, 128, 128], P(('ops', 'sec')), may hold values from -6 to 6
- left_sector: int32 [512], P(('ops', 'sec')), may hold values from 0 to 15, as said below
- right_sector: int32 [512], P(('ops', 'sec')), may hold values from 0 to 1
- left_size: int32 [16], replicated, may hold values from 64 to 128
- right_size: int32 [2], replicated, may hold values from 64 to 128
- left_ops: float32 [16, 4, 128, 128], P('sec', 'ops'), may hold values from -0.25 to 0.25
- right_ops: float32 [2, 4, 128, 128], P(None, 'ops'), may hold values from -0.5 to 0.5
Outputs:
- sigma: float32 [512, 128, 128], P(('ops', 'sec'))
Inputs may be any that keep to these rules, and one draw needn't show every extreme that they name: `left_sector`: the left sectors of the 16 blocks of one device are distinct and come in whole groups g * 2 to g * 2 + 1.
All inputs are finite; a program needn't handle non-finite values.
Results may differ from a plain program's by a relative error of at most 0.0003.
Values sent between devices are 32-bit elements; how exact they have to be, the bound alone decides.
A program may use at most 64 MiB of HBM per device.

v0:
```python
import jax
import jax.numpy as jnp
from jax import lax
from jax.sharding import PartitionSpec as P


def contract(running, packed, left_ids, right_ids, live_count, left_blocks, right_blocks):
    turn_count = (live_count + 1) // 2

    def advance(turn_index, current):
        first = 2 * turn_index
        block = lax.dynamic_slice_in_dim(packed, first, 2, 0)
        left_sel = lax.dynamic_slice_in_dim(left_ids, first, 2, 0)
        right_sel = lax.dynamic_slice_in_dim(right_ids, first, 2, 0)
        left_pick = left_blocks[left_sel]
        right_pick = right_blocks[right_sel]
        halfway = jnp.einsum("sij,stlj->stil", block, right_pick, precision=lax.Precision.HIGHEST)
        update = jnp.einsum("stmi,stil->sml", left_pick, halfway, precision=lax.Precision.HIGHEST)
        before = lax.dynamic_slice_in_dim(current, first, 2, 0)
        return lax.dynamic_update_slice_in_dim(current, before + update, first, 0)

    return lax.fori_loop(0, turn_count, advance, running)


def gather_whole(left_ops, right_ops):
    return (
        lax.all_gather(left_ops, "ops", axis=1, tiled=True),
        lax.all_gather(right_ops, "ops", axis=1, tiled=True),
    )


def arrange(incoming, tags, slot_count, width):
    incoming = incoming.reshape(slot_count, width, width)
    tag_ids = tags.reshape(slot_count).astype(jnp.int32)
    live_flag = (tag_ids > 0).astype(jnp.int32)
    order = jnp.argsort(1 - live_flag, stable=True)
    live_count = jnp.sum(live_flag)
    packed = incoming[order]
    right_ids = jnp.maximum(tag_ids[order] - 1, 0)
    return (packed, right_ids, order, live_count)


def shards(wavefunction, left_sector, right_sector, left_size, right_size, left_ops, right_ops):
    peer_count = lax.axis_size("sec")
    sec_local = left_ops.shape[0]
    width = wavefunction.shape[1]
    position = jnp.arange(width)
    left_live = jnp.sum(
        jnp.where(
            left_sector[:, None] == jnp.arange(left_size.shape[0])[None, :], left_size[None, :], 0
        ),
        axis=1,
    )
    right_live = jnp.sum(
        jnp.where(
            right_sector[:, None] == jnp.arange(right_size.shape[0])[None, :],
            right_size[None, :],
            0,
        ),
        axis=1,
    )
    row_live = position[None, :] < left_live[:, None]
    col_live = position[None, :] < right_live[:, None]
    window = (row_live[:, :, None] & col_live[:, None, :]).astype(jnp.float32)
    masked = wavefunction * window
    owner = left_sector // sec_local
    within = left_sector % sec_local
    outgoing = (
        jnp.zeros((peer_count, sec_local, width, width), jnp.float32).at[owner, within].set(masked)
    )
    labels = (
        jnp.zeros((peer_count, sec_local), jnp.float32)
        .at[owner, within]
        .set((right_sector + 1).astype(jnp.float32))
    )
    incoming, tags = (
        lax.all_to_all(outgoing, "sec", split_axis=0, concat_axis=0, tiled=True),
        lax.all_to_all(labels, "sec", split_axis=0, concat_axis=0, tiled=True),
    )
    slot_count = peer_count * sec_local
    packed, right_ids, order, live_count = arrange(incoming, tags, slot_count, width)
    left_ids = order % sec_local
    empty = jnp.zeros_like(packed)
    left_all, right_all = gather_whole(left_ops, right_ops)
    result = contract(empty, packed, left_ids, right_ids, live_count, left_all, right_all)
    restored = jnp.zeros_like(result).at[order].set(result)
    returned = lax.all_to_all(
        restored.reshape(peer_count, sec_local, width, width),
        "sec",
        split_axis=0,
        concat_axis=0,
        tiled=True,
    )
    return returned[owner, within] * window


def solution(mesh):
    placed = (
        P(("ops", "sec"), None, None),
        P(("ops", "sec")),
        P(("ops", "sec")),
        P(),
        P(),
        P("sec", "ops", None, None),
        P(None, "ops", None, None),
    )
    return jax.shard_map(
        shards, mesh=mesh, in_specs=placed, out_specs=P(("ops", "sec"), None, None), check_vma=False
    )
```

profile of v0, /device:TPU:0, one launch (start us, length us, event | category | flops | bytes accessed | tf_op | source)
XLA Modules:
  0.0 106.0 jit_solution(9594237062470781064)
XLA Ops:
  0.0 0.8 fusion.13
  0.8 1.3 %scatter_fusion = f32[8,2]{0,1:T(2,128)S(1)} fusion(f32[8,2]{0,1:T(2,128)S(1)} %broadcast.79, s32[16]{0:T(128)S(1)} %get-tuple-element.72, f32[16]{0:T(128)S(1)} %add_convert_fusion), kind=kCustom, calls=%fused_computation.5 | custom fusion | bytes 320 | tf_op jit(solution)/shard_map/scatter | solution.py:74
  2.1 0.7 copy.13
  2.8 5.3 %all-to-all-start = ((f32[8,1,2]{2,1,0:T(1,128)}), f32[8,1,2]{2,1,0:T(1,128)S(1)}, u32[]{:S(2)}, u32[]{:S(2)}) async-start(f32[8,1,2]{2,1,0:T(1,128)} %copy.13), calls=%async_computation | async-start | bytes 8192 | tf_op jit(solution)/shard_map/all_to_all | solution.py:78
  8.1 0.1 fusion.6
  8.2 0.5 copy-done.4
  8.8 0.2 select_reduce_fusion
  9.0 16.7 %all_gather.6 = f32[2,4,128,128]{3,2,1,0:T(8,128)S(1)} all-gather(f32[2,1,128,128]{3,2,1,0:T(8,128)} %param.14), channel_id=1, replica_groups=mesh['ops'=4,'sec'=8] {'ops'}, dimensions={1}, use_global_device_ids=true | all-gather | bytes 655360 | tf_op jit(solution)/shard_map/all_gather | solution.py:27
  25.7 0.3 and_select_fusion.1
  26.1 1.1 %broadcast_in_dim.67 = f32[8,2,128,128]{3,2,1,0:T(8,128)} broadcast(f32[]{:T(128)} %constant.60.clone.1), dimensions={} | broadcast | bytes 1048580 | tf_op jit(solution)/shard_map/broadcast_in_dim | solution.py:69
  27.1 3.1 %scatter_fusion.1 = f32[8,2,128,128]{3,2,1,0:T(8,128)} fusion(f32[8,2,128,128]{3,2,1,0:T(8,128)} %broadcast_in_dim.67, s32[16]{0:T(128)S(1)} %get-tuple-element.72, f32[16,128,128]{2,1,0:T(8,128)S(1)} %and_select_fusion.1), kind=kCustom, calls=%fused_computation.6 | custom fusion | bytes 3145856 | tf_op jit(solution)/shard_map/scatter | solution.py:69
  30.3 3.9 %all-to-all-start.1 = ((f32[8,2,128,128]{3,2,1,0:T(8,128)}), f32[8,2,128,128]{3,2,1,0:T(8,128)S(1)}, u32[]{:S(2)}, u32[]{:S(2)}) async-start(f32[8,2,128,128]{3,2,1,0:T(8,128)} %scatter_fusion.1), calls=%async_computation.1 | async-start | bytes 2097152 | tf_op jit(solution)/shard_map/all_to_all | solution.py:77
  34.2 16.8 %all_gather.7 = f32[2,4,128,128]{3,2,1,0:T(8,128)S(1)} all-gather(f32[2,1,128,128]{3,2,1,0:T(8,128)S(1)} %copy-done.1), channel_id=1, replica_groups=mesh['ops'=4,'sec'=8] {'ops'}, dimensions={1}, use_global_device_ids=true | all-gather | bytes 655360 | tf_op jit(solution)/shard_map/all_gather | solution.py:28
  51.0 0.7 fusion.5
  52.5 1.3 %sort.17 = (s32[16]{0:T(128)}, s32[16]{0:T(128)S(1)}) sort(s32[16]{0:T(128)S(1)} %fusion.8, s32[16]{0:T(128)S(1)} %iota.23), dimensions={0}, to_apply=%region_3.4 | sort | flops 64 | bytes 256 | tf_op jit(solution)/shard_map/jit(argsort)/sort | solution.py:36
  53.9 0.7 gather_fusion.2
  54.5 1.6 %gather_fusion.3 = f32[16,128,128]{2,1,0:T(8,128)} fusion(f32[16,128,128]{2,1,0:T(8,128)S(1)} %bitcast.58, s32[1024]{0:T(1024)S(1)} %pad_clamp_fusion.2), kind=kCustom, calls=%fused_computation.3 | custom fusion | bytes 2097216 | tf_op jit(solution)/shard_map/gather | solution.py:38
  56.1 0.1 broadcast.77.clone
  56.2 27.7 %while.10 = (s32[]{:T(128)}, f32[16,128,128]{2,1,0:T(8,128)S(1)}, s32[]{:T(128)}, s32[16]{0:T(128)S(1)}, f32[2,4,128,128]{3,2,1,0:T(8,128)S(1)}, /*index=5*/s32[...) while((s32[]{:T(128)}, f32[16,128,128]{2,1,0:T(8,128)S(1)}, ...), condition=%wide.region_7.8_spmd, body=%wide.region_6.7_spmd.sunk | while | flops 402688000 | bytes 4595951 | solution.py:22
  56.3 0.1 compare_select_fusion.12
  56.3 0.6 gather_fusion.1
  56.9 1.5 %convolution_bitcast_fusion.3 = f32[2,4,128,128]{2,3,1,0:T(8,128)S(1)} fusion(f32[2,4,128,128]{3,2,1,0:T(8,128)S(1)} %gather_fusion.1, f32[16,128,128]{2,1,0:T(8,128)} %get-tuple-element.162, s32[]{:T(128)S(6)} %select_n.122), kind=kOutput, calls=%fused_computation.8.clone.1 | convolution fusion | flops 201326592 | bytes 1179652 | tf_op jit(solution)/shard_map/while/body/sij,stlj->stil/dot_general | solution.py:17
  58.5 0.6 gather_fusion
  59.0 0.6 fusion.26
  59.7 0.1 compare_select_fusion.12
  59.8 0.6 gather_fusion.1
  60.4 1.5 %convolution_bitcast_fusion.3 = f32[2,4,128,128]{2,3,1,0:T(8,128)S(1)} fusion(f32[2,4,128,128]{3,2,1,0:T(8,128)S(1)} %gather_fusion.1, f32[16,128,128]{2,1,0:T(8,128)} %get-tuple-element.162, s32[]{:T(128)S(6)} %select_n.122), kind=kOutput, calls=%fused_computation.8.clone.1 | convolution fusion | flops 201326592 | bytes 1179652 | tf_op jit(solution)/shard_map/while/body/sij,stlj->stil/dot_general | solution.py:17
  61.9 0.6 gather_fusion
  62.5 0.6 fusion.26
  63.2 0.1 compare_select_fusion.12
  63.3 0.6 gather_fusion.1
  63.9 1.5 %convolution_bitcast_fusion.3 = f32[2,4,128,128]{2,3,1,0:T(8,128)S(1)} fusion(f32[2,4,128,128]{3,2,1,0:T(8,128)S(1)} %gather_fusion.1, f32[16,128,128]{2,1,0:T(8,128)} %get-tuple-element.162, s32[]{:T(128)S(6)} %select_n.122), kind=kOutput, calls=%fused_computation.8.clone.1 | convolution fusion | flops 201326592 | bytes 1179652 | tf_op jit(solution)/shard_map/while/body/sij,stlj->stil/dot_general | solution.py:17
  65.4 0.6 gather_fusion
  66.0 0.6 fusion.26
  66.6 0.1 compare_select_fusion.12
  66.7 0.6 gather_fusion.1
  67.3 1.5 %convolution_bitcast_fusion.3 = f32[2,4,128,128]{2,3,1,0:T(8,128)S(1)} fusion(f32[2,4,128,128]{3,2,1,0:T(8,128)S(1)} %gather_fusion.1, f32[16,128,128]{2,1,0:T(8,128)} %get-tuple-element.162, s32[]{:T(128)S(6)} %select_n.122), kind=kOutput, calls=%fused_computation.8.clone.1 | convolution fusion | flops 201326592 | bytes 1179652 | tf_op jit(solution)/shard_map/while/body/sij,stlj->stil/dot_general | solution.py:17
  68.8 0.6 gather_fusion
  69.4 0.6 fusion.26
  70.1 0.1 compare_select_fusion.12
  70.2 0.6 gather_fusion.1
  70.8 1.5 %convolution_bitcast_fusion.3 = f32[2,4,128,128]{2,3,1,0:T(8,128)S(1)} fusion(f32[2,4,128,128]{3,2,1,0:T(8,128)S(1)} %gather_fusion.1, f32[16,128,128]{2,1,0:T(8,128)} %get-tuple-element.162, s32[]{:T(128)S(6)} %select_n.122), kind=kOutput, calls=%fused_computation.8.clone.1 | convolution fusion | flops 201326592 | bytes 1179652 | tf_op jit(solution)/shard_map/while/body/sij,stlj->stil/dot_general | solution.py:17
  72.3 0.6 gather_fusion
  72.9 0.6 fusion.26
  73.6 0.1 compare_select_fusion.12
  73.6 0.6 gather_fusion.1
  74.2 1.5 %convolution_bitcast_fusion.3 = f32[2,4,128,128]{2,3,1,0:T(8,128)S(1)} fusion(f32[2,4,128,128]{3,2,1,0:T(8,128)S(1)} %gather_fusion.1, f32[16,128,128]{2,1,0:T(8,128)} %get-tuple-element.162, s32[]{:T(128)S(6)} %select_n.122), kind=kOutput, calls=%fused_computation.8.clone.1 | convolution fusion | flops 201326592 | bytes 1179652 | tf_op jit(solution)/shard_map/while/body/sij,stlj->stil/dot_general | solution.py:17
  75.8 0.6 gather_fusion
  76.4 0.6 fusion.26
  77.0 0.1 compare_select_fusion.12
  77.1 0.6 gather_fusion.1
  77.7 1.5 %convolution_bitcast_fusion.3 = f32[2,4,128,128]{2,3,1,0:T(8,128)S(1)} fusion(f32[2,4,128,128]{3,2,1,0:T(8,128)S(1)} %gather_fusion.1, f32[16,128,128]{2,1,0:T(8,128)} %get-tuple-element.162, s32[]{:T(128)S(6)} %select_n.122), kind=kOutput, calls=%fused_computation.8.clone.1 | convolution fusion | flops 201326592 | bytes 1179652 | tf_op jit(solution)/shard_map/while/body/sij,stlj->stil/dot_general | solution.py:17
  79.2 0.6 gather_fusion
  79.8 0.6 fusion.26
  80.5 0.1 compare_select_fusion.12
  80.6 0.6 gather_fusion.1
  81.2 1.5 %convolution_bitcast_fusion.3 = f32[2,4,128,128]{2,3,1,0:T(8,128)S(1)} fusion(f32[2,4,128,128]{3,2,1,0:T(8,128)S(1)} %gather_fusion.1, f32[16,128,128]{2,1,0:T(8,128)} %get-tuple-element.162, s32[]{:T(128)S(6)} %select_n.122), kind=kOutput, calls=%fused_computation.8.clone.1 | convolution fusion | flops 201326592 | bytes 1179652 | tf_op jit(solution)/shard_map/while/body/sij,stlj->stil/dot_general | solution.py:17
  82.7 0.6 gather_fusion
  83.3 0.6 fusion.26
  83.9 0.1 broadcast.77
  84.0 1.1 %scatter_fusion.2 = f32[16,128,128]{2,1,0:T(8,128)S(1)} fusion(f32[16,128,128]{2,1,0:T(8,128)S(1)} %broadcast.77, s32[16]{0:T(128)S(1)} %get-tuple-element.74, f32[16,128,128]{2,1,0:T(8,128)S(1)} %get-tuple-element.50), kind=kCustom, calls=%fused_computation.7 | custom fusion | bytes 3145792 | tf_op jit(solution)/shard_map/scatter | solution.py:86
  85.2 18.9 %all_to_all.19 = f32[8,2,128,128]{3,2,1,0:T(8,128)S(1)} all-to-all(f32[8,2,128,128]{3,2,1,0:T(8,128)S(1)} %bitcast.57), channel_id=1, replica_groups=mesh['ops'=4,'sec'=8] {'sec'}, dimensions={0} | all-to-all | bytes 2097152 | tf_op jit(solution)/shard_map/all_to_all | solution.py:87
  104.1 0.6 gather_fusion.4
  104.7 1.3 %and_select_fusion = f32[16,128,128]{2,1,0:T(8,128)} fusion(f32[16,128,128]{2,1,0:T(8,128)S(1)} %gather_fusion.4, pred[16,128]{1,0:T(8,128)(4,1)S(1)} %get-tuple-element.75, pred[16,128]{1,0:T(8,128)(4,1)S(1)} %get-tuple-element.76), kind=kLoop, calls=%fused_computation.19 | loop fusion | flops 524288 | bytes 2101248 | tf_op jit(solution)/shard_map/mul | solution.py:94
  (38 shorter events, 0.3 us)
Async XLA Ops:
  0.0 0.8 copy-start.2
  0.0 25.7 %copy-start = (f32[16,128,128]{2,1,0:T(8,128)S(1)}, f32[16,128,128]{2,1,0:T(8,128)}, u32[]{:S(2)}) copy-start(f32[16,128,128]{2,1,0:T(8,128)} %param.9) | copy-start | bytes 3145732
  2.8 5.3 %copy-start.3 = (s32[2]{0:T(128)S(1)}, s32[2]{0:T(128)}, u32[]{:S(2)}) copy-start(s32[2]{0:T(128)} %param.13) | copy-start | bytes 28
  2.8 27.5 %all-to-all-start = ((f32[8,1,2]{2,1,0:T(1,128)}), f32[8,1,2]{2,1,0:T(1,128)S(1)}, u32[]{:S(2)}, u32[]{:S(2)}) async-start(f32[8,1,2]{2,1,0:T(1,128)} %copy.13), calls=%async_computation | async-start | bytes 8192 | tf_op jit(solution)/shard_map/all_to_all | solution.py:78
  8.1 0.7 copy-start.4
  8.1 0.7 copy-start.5
  30.2 4.0 %copy-start.1 = (f32[2,1,128,128]{3,2,1,0:T(8,128)S(1)}, f32[2,1,128,128]{3,2,1,0:T(8,128)}, u32[]{:S(2)}) copy-start(f32[2,1,128,128]{3,2,1,0:T(8,128)} %param.15) | copy-start | bytes 393220
  30.3 24.3 %all-to-all-start.1 = ((f32[8,2,128,128]{3,2,1,0:T(8,128)}), f32[8,2,128,128]{3,2,1,0:T(8,128)S(1)}, u32[]{:S(2)}, u32[]{:S(2)}) async-start(f32[8,2,128,128]{3,2,1,0:T(8,128)} %scatter_fusion.1), calls=%async_computation.1 | async-start | bytes 2097152 | tf_op jit(solution)/shard_map/all_to_all | solution.py:77
where the time goes:
time: 107 us; the launch traced here: 106 us
  blocking collectives  52.4 us (49%)
  local copies, waits for them, and re-layouts  20.3 us (19%)
  matrix products  17.1 us (16%)
  starting transfers between devices  9.27 us (9%)
  other arithmetic  5.58 us (5%)
    all_to_all x1, blocking collectives, shards(): lax.all_to_all(restored.reshape(peer_count, sec_local, width, width), 'se...  18.9 us
    all_gather x1, blocking collectives, gather_whole(): lax.all_gather(right_ops, 'ops', axis=1, tiled=True)  16.8 us
    all_gather x1, blocking collectives, gather_whole(): lax.all_gather(left_ops, 'ops', axis=1, tiled=True)  16.7 us
    dot_general x8, matrix products, advance(): jnp.einsum('sij,stlj->stil', block, right_pick, precision=lax.Precision.H...  12 us
    all_to_all x1, starting transfers between devices, shards(): lax.all_to_all(labels, 'sec', split_axis=0, concat_axis=0, tiled=True)  5.33 us
    dot_general x8, matrix products, advance(): jnp.einsum('stmi,stil->sml', left_pick, halfway, precision=lax.Precision....  5.1 us
    gather x8, local copies, waits for them, and re-layouts, advance(): right_pick = right_blocks[right_sel]  4.66 us
    gather x8, local copies, waits for them, and re-layouts, advance(): left_pick = left_blocks[left_sel]  4.66 us
  transfers between devices with their start and end apart: 2, of which 0 were waited for; matrix products, arithmetic and copies ran while one was open for 7% of the time, Pallas kernels for 0%

commit v1 on v0

--- a/solution.py
+++ b/solution.py
@@ -1,7 +1,11 @@
 import jax
 import jax.numpy as jnp
 from jax import lax
+from jax.experimental import pallas as pl
+from jax.experimental.pallas import tpu as pltpu
 from jax.sharding import PartitionSpec as P
+
+MESH = pl.DeviceIdType.MESH
 
 
 def contract(running, packed, left_ids, right_ids, live_count, left_blocks, right_blocks):
@@ -94,6 +98,310 @@
     return returned[owner, within] * window
 
 
+def term_orders(count):
+    orders = []
+    for here in range(count):
+        orders.append(sorted(range(count), key=lambda t: (abs(t - here), abs(2 * t - count + 1), t)))
+    return orders
+
+
+def split(value):
+    high = value.astype(jnp.bfloat16)
+    low = (value - high.astype(jnp.float32)).astype(jnp.bfloat16)
+    return high, low
+
+
+def gather_contract(
+    wf_hbm, lops_hbm, rops_hbm, lsec, rsec, lsize, rsize,
+    out_ref,
+    wbuf, lbuf, rbuf, mcat, hcat, acc, inverse, right_of,
+    own_sem, recv_l, recv_r, send_x, send_y, send_up, send_dn, send_sib,
+):
+    terms = lax.axis_size("ops")
+    sectors, _, width, _ = lbuf.shape
+    rights = rbuf.shape[1]
+    half = width // 2
+    z = lax.axis_index("ops")
+    sec = lax.axis_index("sec")
+    core = sec % 2
+    xpos = (sec // 2) % 2
+    ypos = sec // 4
+    sib = sec + 1 - 2 * core
+    xnb = sec + 2 - 4 * xpos
+    ynb = sec + 4 - 8 * ypos
+    dnb = xnb + 4 - 8 * ypos
+    has_up = z < terms - 1
+    has_dn = z > 0
+    table = term_orders(terms)
+    order = []
+    for k in range(terms):
+        value = table[0][k] * 1
+        for here in range(1, terms):
+            value = jnp.where(z == here, table[here][k], value)
+        order.append(value)
+
+    def flip(group):
+        return group + 1 - 2 * core
+
+    barrier = pltpu.get_barrier_semaphore()
+
+    def greet(zz, ss):
+        pl.semaphore_signal(barrier, inc=1, device_id=(zz, ss), device_id_type=MESH)
+
+    for peer in (sib, xnb, ynb):
+        greet(z, peer)
+
+    @pl.when(has_up)
+    def _():
+        greet(z + 1, sec)
+
+    @pl.when(has_dn)
+    def _():
+        greet(z - 1, sec)
+
+    own_l = [
+        pltpu.make_async_copy(lops_hbm.at[i, 0], lbuf.at[2 * sec + i, z], recv_l.at[2 * sec + i, z])
+        for i in range(2)
+    ]
+    own_r = pltpu.make_async_copy(rops_hbm.at[:, 0], rbuf.at[z], own_sem.at[0])
+    own_w = pltpu.make_async_copy(wf_hbm, wbuf, own_sem.at[1])
+    own_w.start()
+    own_r.start()
+    for copy in own_l:
+        copy.start()
+    pl.semaphore_wait(barrier, 3 + has_up.astype(jnp.int32) + has_dn.astype(jnp.int32))
+
+    def move(src, dst, ssem, rsem, zz, ss):
+        return pltpu.make_async_remote_copy(
+            src_ref=src, dst_ref=dst, send_sem=ssem, recv_sem=rsem,
+            device_id=(zz, ss), device_id_type=MESH,
+        )
+
+    def piece(group, i, t, ssem, zz, ss, own=False):
+        s = 2 * group + i
+        src = lops_hbm.at[i, 0] if own else lbuf.at[s, t]
+        return move(src, lbuf.at[s, t], ssem, recv_l.at[s, t], zz, ss)
+
+    def rpiece(h, t, ssem, zz, ss, own=False):
+        rows = pl.ds(pl.multiple_of(h * half, half), half)
+        src = rops_hbm.at[:, 0, rows] if own else rbuf.at[t, :, rows]
+        return move(src, rbuf.at[t, :, rows], ssem, recv_r.at[t, h], zz, ss)
+
+    def await_l(group, i, t):
+        piece(group, i, t, send_x.at[t, 0], z, xnb).wait_recv()
+
+    def await_r(h, t):
+        rpiece(h, t, send_x.at[t, 0], z, xnb).wait_recv()
+
+    def along(make, j, t, own, act):
+        up = has_up & (t <= z)
+        dn = has_dn & (t >= z)
+
+        @pl.when(up)
+        def _():
+            act(make(t, send_up.at[t, j], z + 1, sec, own))
+
+        @pl.when(dn)
+        def _():
+            act(make(t, send_dn.at[t, j], z - 1, sec, own))
+
+    def fan_own(i, t, own, act):
+        along(lambda t, ssem, zz, ss, own: piece(sec, i, t, ssem, zz, ss, own), i, t, own, act)
+        act(piece(sec, i, t, send_x.at[t, i], z, xnb, own))
+        act(piece(sec, i, t, send_y.at[t, i], z, ynb, own))
+        act(piece(sec, i, t, send_sib.at[t, i], z, sib, own))
+
+    def fan_right(t, own, act):
+        along(lambda t, ssem, zz, ss, own: rpiece(core, t, ssem, zz, ss, own), 2, t, own, act)
+        if not own:
+            act(rpiece(core, t, send_sib.at[t, 8], z, sib))
+
+    def fan_x(i, t, act):
+        if i == 0:
+            act(piece(xnb, i, t, send_y.at[t, 2], z, ynb))
+        act(piece(xnb, i, t, send_sib.at[t, 2 + i], z, sib))
+
+    def fan_y(i, t, act):
+        if i == 1:
+            act(piece(ynb, i, t, send_x.at[t, 2], z, xnb))
+        act(piece(ynb, i, t, send_sib.at[t, 4 + i], z, sib))
+
+    def fan_d(i, t, act):
+        act(piece(dnb, i, t, send_sib.at[t, 6 + i], z, sib))
+
+    start = lambda copy: copy.start()
+    drain = lambda copy: copy.wait_send()
+
+    t0 = order[0]
+    for i in range(2):
+        fan_own(i, t0, True, start)
+    fan_right(t0, True, start)
+
+    for s in range(sectors):
+        value = jnp.int32(0)
+        for p in range(1, sectors):
+            value = jnp.where(lsec[p] == s, p, value)
+        inverse[s] = value
+        right_of[s] = rsec[value]
+
+    row_at = lax.broadcasted_iota(jnp.int32, (width, width), 0)
+    col_at = lax.broadcasted_iota(jnp.int32, (width, width), 1)
+
+    own_w.wait()
+
+    @pl.loop(0, sectors)
+    def _(s):
+        live = (row_at < lsize[s]) & (col_at < rsize[right_of[s]])
+        high, low = split(jnp.where(live, wbuf[inverse[s]], 0.0))
+        rows = pl.ds(pl.multiple_of(s * width, width), width)
+        mcat[rows, :width] = high
+        mcat[rows, width:] = low
+        acc[s] = jnp.zeros((width, width), jnp.float32)
+
+    own_r.wait()
+    batch = 4 if sectors % 4 == 0 else 1
+
+    def halfway(t):
+        high, low = split(rbuf[t].reshape(rights * width, width))
+        doubled = jnp.concatenate([high, high], axis=1)
+        contract_last = (((1,), (1,)), ((), ()))
+
+        @pl.loop(0, sectors // batch)
+        def _(n):
+            rows = pl.ds(pl.multiple_of(n * batch * width, batch * width), batch * width)
+            left = mcat[rows, :]
+            both = lax.dot_general(left, doubled, contract_last, preferred_element_type=jnp.float32)
+            both += lax.dot_general(
+                left[:, :width], low, contract_last, preferred_element_type=jnp.float32
+            )
+            for j in range(batch):
+                s = n * batch + j
+                mine = both[j * width : (j + 1) * width]
+                which = jnp.full((width, width), right_of[s], jnp.int32)
+                pick = mine[:, :width]
+                for b in range(1, rights):
+                    pick = jnp.where(which == b, mine[:, b * width : (b + 1) * width], pick)
+                h_high, h_low = split(pick)
+                hcat[t, s, :, :width] = h_high
+                hcat[t, s, :, width:] = h_low
+
+    def apply_left(s, t):
+        high, low = split(lbuf[s, t])
+        wide = jnp.dot(
+            jnp.concatenate([high, low], axis=0), hcat[t, s], preferred_element_type=jnp.float32
+        )
+        acc[s] += wide[:width, :width] + (wide[:width, width:] + wide[width:, :width])
+
+    def apply_group(group, t, wait):
+        if wait:
+            for i in range(2):
+                await_l(group, i, t)
+        for i in range(2):
+            apply_left(2 * group + i, t)
+
+    for k in range(terms + 2):
+        if 1 <= k < terms:
+            for i in range(2):
+                await_l(sec, i, order[k])
+                fan_own(i, order[k], False, start)
+        if 1 <= k <= terms:
+            t = order[k - 1]
+            for i in range(2):
+                await_l(xnb, i, t)
+                fan_x(i, t, start)
+                await_l(ynb, i, t)
+                fan_y(i, t, start)
+        if 2 <= k:
+            t = order[k - 2]
+            for i in range(2):
+                await_l(dnb, i, t)
+                fan_d(i, t, start)
+        if 1 <= k < terms:
+            await_r(core, order[k])
+            fan_right(order[k], False, start)
+        if 1 <= k <= terms:
+            t = order[k - 1]
+            apply_group(xnb, t, False)
+            apply_group(ynb, t, False)
+            apply_group(flip(xnb), t, True)
+            apply_group(flip(ynb), t, True)
+        if 2 <= k:
+            t = order[k - 2]
+            apply_group(dnb, t, False)
+            apply_group(flip(dnb), t, True)
+        if k < terms:
+            t = order[k]
+            if k >= 1:
+                await_r(1 - core, t)
+            else:
+                for copy in own_l:
+                    copy.wait()
+            halfway(t)
+            apply_group(sec, t, False)
+            apply_group(sib, t, True)
+
+    @pl.loop(0, sectors)
+    def _(p):
+        s = lsec[p]
+        live = (row_at < lsize[s]) & (col_at < rsize[rsec[p]])
+        out_ref[p] = jnp.where(live, acc[s], 0.0)
+
+    for k in range(terms):
+        t = order[k]
+        for i in range(2):
+            fan_own(i, t, k == 0, drain)
+            fan_x(i, t, drain)
+            fan_y(i, t, drain)
+            fan_d(i, t, drain)
+        fan_right(t, k == 0, drain)
+
+
+def local_shards(wavefunction, left_sector, right_sector, left_size, right_size, left_ops, right_ops):
+    terms = lax.axis_size("ops")
+    sectors, width = left_size.shape[0], wavefunction.shape[1]
+    rights = right_size.shape[0]
+    dma = pltpu.SemaphoreType.DMA
+    anywhere = pl.BlockSpec(memory_space=pl.ANY)
+    scalars = pl.BlockSpec(memory_space=pltpu.SMEM)
+    return pl.pallas_call(
+        gather_contract,
+        out_shape=jax.ShapeDtypeStruct(wavefunction.shape, jnp.float32),
+        in_specs=[anywhere] * 3 + [scalars] * 4,
+        out_specs=pl.BlockSpec(memory_space=pltpu.VMEM),
+        scratch_shapes=[
+            pltpu.VMEM((sectors, width, width), jnp.float32),
+            pltpu.VMEM((sectors, terms, width, width), jnp.float32),
+            pltpu.VMEM((terms, rights, width, width), jnp.float32),
+            pltpu.VMEM((sectors * width, 2 * width), jnp.bfloat16),
+            pltpu.VMEM((terms, sectors, width, 2 * width), jnp.bfloat16),
+            pltpu.VMEM((sectors, width, width), jnp.float32),
+            pltpu.SMEM((sectors,), jnp.int32),
+            pltpu.SMEM((sectors,), jnp.int32),
+            dma((2,)),
+            dma((sectors, terms)),
+            dma((terms, 2)),
+            dma((terms, 3)),
+            dma((terms, 3)),
+            dma((terms, 3)),
+            dma((terms, 3)),
+            dma((terms, 9)),
+        ],
+        compiler_params=pltpu.CompilerParams(collective_id=0, has_side_effects=True),
+    )(wavefunction, left_ops, right_ops, left_sector, right_sector, left_size, right_size)
+
+
+def cube_shards(*arrays):
+    wavefunction, left_size, left_ops = arrays[0], arrays[3], arrays[5]
+    sectors, width = left_size.shape[0], wavefunction.shape[1]
+    terms = lax.axis_size("ops")
+    every_sector = wavefunction.shape[0] == sectors
+    cube = lax.axis_size("sec") == 2**3 and left_ops.shape[:2] == (2, 1)
+    small = sectors * terms * width * width * 4 <= 2**23
+    if every_sector and cube and small:
+        return local_shards(*arrays)
+    return shards(*arrays)
+
+
 def solution(mesh):
     placed = (
         P(("ops", "sec"), None, None),
@@ -105,5 +413,5 @@
         P(None, "ops", None, None),
     )
     return jax.shard_map(
-        shards, mesh=mesh, in_specs=placed, out_specs=P(("ops", "sec"), None, None), check_vma=False
-    )
+        cube_shards, mesh=mesh, in_specs=placed, out_specs=P(("ops", "sec"), None, None), check_vma=False
+    )

time: 107 us -> 36.8 us (0.34)
  blocking collectives: 52.4 us -> 0 us
  Pallas kernels: 0 us -> 34 us
  local copies, waits for them, and re-layouts: 20.3 us -> 2.3 us
  matrix products: 17.1 us -> 0 us
  starting transfers between devices: 9.27 us -> 0 us
  other arithmetic: 5.58 us -> 0 us
    pallas_call x0 -> x1, Pallas kernels: none -> 34 us  [local_shards(): pl.pallas_call(gather_contract, out_shape=jax.ShapeDtypeStruct(wavefuncti...]
    all_gather x2 -> x0, blocking collectives: 33.5 us -> none  [the longest x1 16.8 us: gather_whole(): lax.all_gather(right_ops, 'ops', axis=1, tiled=True)]
    all_to_all x1 -> x0, blocking collectives: 18.9 us -> none  [shards(): lax.all_to_all(restored.reshape(peer_count, sec_local, width, width), 'se...]
    dot_general x16 -> x0, matrix products: 17.1 us -> none  [the longest x8 12 us: advance(): jnp.einsum('sij,stlj->stil', block, right_pick, precision=lax.Precision.H...]
    gather x19 -> x0, local copies, waits for them, and re-layouts: 12.2 us -> none  [the longest x8 4.66 us: advance(): right_pick = right_blocks[right_sel]]
    all_to_all x2 -> x0, starting transfers between devices: 9.27 us -> none  [the longest x1 5.33 us: shards(): lax.all_to_all(labels, 'sec', split_axis=0, concat_axis=0, tiled=True)]
    scatter x3 -> x0, local copies, waits for them, and re-layouts: 5.52 us -> none  [the longest x1 3.11 us: shards(): jnp.zeros((peer_count, sec_local, width, width), jnp.float32)]
    unnamed x12 -> x1, local copies, waits for them, and re-layouts: 0.59 us -> 2.3 us
  transfers between devices with their start and end apart: 2 -> 0, of which waited for: 0 -> 0; matrix products, arithmetic and copies ran while one was open for 7% -> 0% of each run, Pallas kernels for 0% -> 0%
where the time goes in v1:
time: 36.8 us; the launch traced here: 36.3 us
  Pallas kernels  34 us (92%)
  local copies, waits for them, and re-layouts  2.3 us (6%)
    pallas_call x1, Pallas kernels, local_shards(): pl.pallas_call(gather_contract, out_shape=jax.ShapeDtypeStruct(wavefuncti...  34 us
    unnamed x1, local copies, waits for them, and re-layouts  2.3 us

profile of v1, /device:TPU:0, one launch (start us, length us, event | category | flops | bytes accessed | tf_op | source)
XLA Modules:
  0.0 36.3 jit_solution(16533293111606193349)
XLA Ops:
  0.0 34.0 %shard_map.73 = f32[16,128,128]{2,1,0:T(8,128)} custom-call(f32[16,128,128]{2,1,0:T(8,128)} %wf_hbm.1, f32[2,1,128,128]{3,2,1,0:T(8,128)} %lops_hbm.1, f32[2,1,128,128]{3,2,1,0:T(8,128)} %rops_hbm.1, s32[16]{0:T(128)} %lsec.1, s32[16]{0:T(128)} %rsec.1, s32[16]{0:T(128)} %lsize.1, s32[2]{0:T(128)} %rsize.1), custom_call_target="tpu_custom_call" | custom-call | tf_op jit(solution)/shard_map/pallas_call | solution.py:366
  34.0 2.3 %copy.9 = f32[16,128,128]{2,1,0:T(8,128)} copy(f32[16,128,128]{2,1,0:T(8,128)} %shard_map.73) | data formatting | bytes 2097152

commit v2 on v1

--- a/solution.py
+++ b/solution.py
@@ -299,46 +299,113 @@
         for i in range(2):
             apply_left(2 * group + i, t)
 
-    for k in range(terms + 2):
-        if 1 <= k < terms:
-            for i in range(2):
-                await_l(sec, i, order[k])
-                fan_own(i, order[k], False, start)
-        if 1 <= k <= terms:
-            t = order[k - 1]
-            for i in range(2):
-                await_l(xnb, i, t)
-                fan_x(i, t, start)
-                await_l(ynb, i, t)
-                fan_y(i, t, start)
-        if 2 <= k:
-            t = order[k - 2]
-            for i in range(2):
-                await_l(dnb, i, t)
-                fan_d(i, t, start)
-        if 1 <= k < terms:
-            await_r(core, order[k])
-            fan_right(order[k], False, start)
-        if 1 <= k <= terms:
-            t = order[k - 1]
-            apply_group(xnb, t, False)
-            apply_group(ynb, t, False)
-            apply_group(flip(xnb), t, True)
-            apply_group(flip(ynb), t, True)
-        if 2 <= k:
-            t = order[k - 2]
-            apply_group(dnb, t, False)
-            apply_group(flip(dnb), t, True)
-        if k < terms:
-            t = order[k]
-            if k >= 1:
-                await_r(1 - core, t)
-            else:
-                for copy in own_l:
-                    copy.wait()
-            halfway(t)
-            apply_group(sec, t, False)
-            apply_group(sib, t, True)
+    def land_own(k, i):
+        await_l(sec, i, order[k])
+        fan_own(i, order[k], False, start)
+
+    def land_side(k, i):
+        await_l(xnb, i, order[k])
+        fan_x(i, order[k], start)
+        await_l(ynb, i, order[k])
+        fan_y(i, order[k], start)
+
+    def land_far(k):
+        for i in range(2):
+            await_l(dnb, i, order[k])
+            fan_d(i, order[k], start)
+
+    def land_right(k):
+        await_r(core, order[k])
+        fan_right(order[k], False, start)
+
+    def apply_side(k):
+        apply_group(xnb, order[k], False)
+        apply_group(ynb, order[k], False)
+        apply_group(flip(xnb), order[k], True)
+        apply_group(flip(ynb), order[k], True)
+
+    def apply_far(k):
+        apply_group(dnb, order[k], False)
+        apply_group(flip(dnb), order[k], True)
+
+    def apply_own(k):
+        await_r(1 - core, order[k])
+        halfway(order[k])
+        apply_group(sec, order[k], False)
+        apply_group(sib, order[k], True)
+
+    middle = has_up & has_dn
+    border = jnp.logical_not(middle)
+
+    for copy in own_l:
+        copy.wait()
+    halfway(order[0])
+    apply_group(sec, order[0], False)
+
+    for i in range(2):
+        land_own(1, i)
+        land_side(0, i)
+
+    @pl.when(middle)
+    def _():
+        for i in range(2):
+            land_own(2, i)
+
+    apply_group(sib, order[0], True)
+    apply_side(0)
+    land_right(1)
+    land_side(1, 0)
+    apply_own(1)
+    land_side(1, 1)
+
+    @pl.when(border)
+    def _():
+        for i in range(2):
+            land_own(2, i)
+
+    @pl.when(middle)
+    def _():
+        for i in range(2):
+            land_own(3, i)
+        land_right(2)
+
+    land_far(0)
+    apply_side(1)
+
+    @pl.when(border)
+    def _():
+        for i in range(2):
+            land_own(3, i)
+
+    @pl.when(middle)
+    def _():
+        land_right(3)
+
+    for i in range(2):
+        land_side(2, i)
+    apply_far(0)
+
+    @pl.when(border)
+    def _():
+        land_right(2)
+
+    apply_own(2)
+    for i in range(2):
+        land_side(3, i)
+    apply_side(2)
+
+    @pl.when(border)
+    def _():
+        land_right(3)
+
+    apply_own(3)
+    land_far(1)
+    apply_side(3)
+    land_far(2)
+    apply_far(1)
+    land_far(3)
+    apply_far(2)
+    apply_far(3)
 
     @pl.loop(0, sectors)
     def _(p):
@@ -395,7 +462,7 @@
     sectors, width = left_size.shape[0], wavefunction.shape[1]
     terms = lax.axis_size("ops")
     every_sector = wavefunction.shape[0] == sectors
-    cube = lax.axis_size("sec") == 2**3 and left_ops.shape[:2] == (2, 1)
+    cube = lax.axis_size("sec") == 2**3 and terms == 2**2 and left_ops.shape[:2] == (2, 1)
     small = sectors * terms * width * width * 4 <= 2**23
     if every_sector and cube and small:
         return local_shards(*arrays)

time: 36.8 us -> 35.8 us (0.973)
  Pallas kernels: 34 us -> 33.3 us
    pallas_call x1, Pallas kernels: 34 us -> 33.3 us  [local_shards(): pl.pallas_call(gather_contract, out_shape=jax.ShapeDtypeStruct(wavefuncti...]
where the time goes in v2:
time: 35.8 us; the launch traced here: 35.6 us
  Pallas kernels  33.3 us (93%)
  local copies, waits for them, and re-layouts  2.3 us (6%)
    pallas_call x1, Pallas kernels, local_shards(): pl.pallas_call(gather_contract, out_shape=jax.ShapeDtypeStruct(wavefuncti...  33.3 us
    unnamed x1, local copies, waits for them, and re-layouts  2.3 us

profile of v2, /device:TPU:0, one launch (start us, length us, event | category | flops | bytes accessed | tf_op | source)
XLA Modules:
  0.0 35.6 jit_solution(1194737511629994427)
XLA Ops:
  0.0 33.3 %shard_map.73 = f32[16,128,128]{2,1,0:T(8,128)} custom-call(f32[16,128,128]{2,1,0:T(8,128)} %wf_hbm.1, f32[2,1,128,128]{3,2,1,0:T(8,128)} %lops_hbm.1, f32[2,1,128,128]{3,2,1,0:T(8,128)} %rops_hbm.1, s32[16]{0:T(128)} %lsec.1, s32[16]{0:T(128)} %rsec.1, s32[16]{0:T(128)} %lsize.1, s32[2]{0:T(128)} %rsize.1), custom_call_target="tpu_custom_call" | custom-call | tf_op jit(solution)/shard_map/pallas_call | solution.py:433
  33.3 2.3 %copy.9 = f32[16,128,128]{2,1,0:T(8,128)} copy(f32[16,128,128]{2,1,0:T(8,128)} %shard_map.73) | data formatting | bytes 2097152

commit v3 on v2

--- a/solution.py
+++ b/solution.py
@@ -113,8 +113,8 @@
 
 def gather_contract(
     wf_hbm, lops_hbm, rops_hbm, lsec, rsec, lsize, rsize,
-    out_ref,
-    wbuf, lbuf, rbuf, mcat, hcat, acc, inverse, right_of,
+    out,
+    out_ref, out_sem, wbuf, lbuf, rbuf, mcat, hcat, acc, inverse, right_of,
     own_sem, recv_l, recv_r, send_x, send_y, send_up, send_dn, send_sib,
 ):
     terms = lax.axis_size("ops")
@@ -398,20 +398,20 @@
     def _():
         land_right(3)
 
+    land_far(1)
     apply_own(3)
-    land_far(1)
+    apply_far(1)
+    land_far(2)
     apply_side(3)
-    land_far(2)
-    apply_far(1)
     land_far(3)
     apply_far(2)
     apply_far(3)
 
-    @pl.loop(0, sectors)
-    def _(p):
+    for p in range(sectors):
         s = lsec[p]
         live = (row_at < lsize[s]) & (col_at < rsize[rsec[p]])
         out_ref[p] = jnp.where(live, acc[s], 0.0)
+        pltpu.make_async_copy(out_ref.at[p], out.at[p], out_sem.at[p]).start()
 
     for k in range(terms):
         t = order[k]
@@ -421,6 +421,9 @@
             fan_y(i, t, drain)
             fan_d(i, t, drain)
         fan_right(t, k == 0, drain)
+
+    for p in range(sectors):
+        pltpu.make_async_copy(out_ref.at[p], out.at[p], out_sem.at[p]).wait()
 
 
 def local_shards(wavefunction, left_sector, right_sector, left_size, right_size, left_ops, right_ops):
@@ -434,8 +437,10 @@
         gather_contract,
         out_shape=jax.ShapeDtypeStruct(wavefunction.shape, jnp.float32),
         in_specs=[anywhere] * 3 + [scalars] * 4,
-        out_specs=pl.BlockSpec(memory_space=pltpu.VMEM),
+        out_specs=anywhere,
         scratch_shapes=[
+            pltpu.VMEM(wavefunction.shape, jnp.float32),
+            dma((sectors,)),
             pltpu.VMEM((sectors, width, width), jnp.float32),
             pltpu.VMEM((sectors, terms, width, width), jnp.float32),
             pltpu.VMEM((terms, rights, width, width), jnp.float32),

time: 35.8 us -> 35.2 us (0.983)
  Pallas kernels: 33.3 us -> 32.7 us
    pallas_call x1, Pallas kernels: 33.3 us -> 32.7 us  [local_shards(): pl.pallas_call(gather_contract, out_shape=jax.ShapeDtypeStruct(wavefuncti...]
where the time goes in v3:
time: 35.2 us; the launch traced here: 35 us
  Pallas kernels  32.7 us (93%)
  local copies, waits for them, and re-layouts  2.3 us (7%)
    pallas_call x1, Pallas kernels, local_shards(): pl.pallas_call(gather_contract, out_shape=jax.ShapeDtypeStruct(wavefuncti...  32.7 us
    unnamed x1, local copies, waits for them, and re-layouts  2.3 us

profile of v3, /device:TPU:0, one launch (start us, length us, event | category | flops | bytes accessed | tf_op | source)
XLA Modules:
  0.0 35.0 jit_solution(6579667101868657176)
XLA Ops:
  0.0 32.7 %shard_map.73 = f32[16,128,128]{2,1,0:T(8,128)} custom-call(f32[16,128,128]{2,1,0:T(8,128)} %wf_hbm.1, f32[2,1,128,128]{3,2,1,0:T(8,128)} %lops_hbm.1, f32[2,1,128,128]{3,2,1,0:T(8,128)} %rops_hbm.1, s32[16]{0:T(128)} %lsec.1, s32[16]{0:T(128)} %rsec.1, s32[16]{0:T(128)} %lsize.1, s32[2]{0:T(128)} %rsize.1), custom_call_target="tpu_custom_call" | custom-call | tf_op jit(solution)/shard_map/pallas_call | solution.py:436
  32.7 2.3 %copy.9 = f32[16,128,128]{2,1,0:T(8,128)} copy(f32[16,128,128]{2,1,0:T(8,128)} %shard_map.73) | data formatting | bytes 2097152
